TPU v7x, 512 devices: a whole 4x8x8 slice. The times are simulated.
512 devices in a mesh: tgt: 16 (over y, core), src: 32 (over z, x).
Axes of the slice: x: 4, y: 8, z: 8, core: 2. Of those that a mesh axis runs over, the one named last changes fastest.
Arguments:
- trial_vectors: float32 [8, 512, 128], P(None, ('tgt', 'src')), may hold values from -18 to 18
- couplings: float32 [512, 32, 128, 128], P('tgt', 'src'), may hold values from -0.125 to 0.125
- neighbours: int32 [512, 32], P('tgt', 'src'), may hold values from 0 to 511, as said below
- live_slots: int32 [512, 32], P('tgt', 'src'), may hold values from 0 to 1, as said below
- energies: float32 [512, 128], P(('tgt', 'src')), may hold values from 1 to 3
Outputs:
- sigma_vectors: float32 [8, 512, 128], P(None, ('tgt', 'src'))
- residual: float32 [8, 512, 128], P(None, ('tgt', 'src'))
- residual_norms: float32 [8], replicated
Inputs may be any that keep to these rules, and one draw needn't show every extreme that they name: `neighbours`: each entry differs from its own chromophore's index by at most 16. `live_slots`: some chromophore has all 32 slots live.
All inputs are finite; a program needn't handle non-finite values.
Results may differ from a plain program's by a relative error of at most 0.000062.
Values sent between devices are 32-bit elements; how exact they have to be, the bound alone decides.
A program may use at most 64 MiB of HBM per device.

v0:
```python
import jax
import jax.numpy as jnp
from jax import lax
from jax.sharding import PartitionSpec as P


def with_halo(block, sides, width):
    for axis, dim in sides:
        count = lax.axis_size(axis)
        forward = [(i, i + 1) for i in range(count - 1)]
        backward = [(target, source) for source, target in forward]
        low = lax.ppermute(
            lax.slice_in_dim(block, block.shape[dim] - width, None, axis=dim), axis, forward
        )
        high = lax.ppermute(lax.slice_in_dim(block, 0, width, axis=dim), axis, backward)
        block = jnp.concatenate([low, block, high], axis=dim)
    return block


def shards(trial_vectors, couplings, neighbours, live_slots, energies):
    vectors = trial_vectors.shape[0]
    states = trial_vectors.shape[2]
    source_block = lax.all_gather(trial_vectors, "src", axis=1, tiled=True)
    block_len = source_block.shape[1]
    widened = with_halo(source_block, (("tgt", 1),), block_len)
    anchor = lax.axis_index("tgt") * block_len - block_len
    local_rows = neighbours - anchor
    slot_count = neighbours.shape[1]
    fetched = jnp.take(widened, local_rows.reshape(-1), axis=1)
    fetched = fetched.reshape(vectors, block_len, slot_count, states)
    fetched = fetched * live_slots.astype(jnp.float32)[None, :, :, None]
    partial_value = jnp.einsum(
        "inab,kinb->kia", couplings, fetched, precision=lax.Precision.HIGHEST
    )
    sigmas = (
        lax.psum_scatter(partial_value, "src", scatter_dimension=1, tiled=True)
        + energies[None] * trial_vectors
    )
    projected = jnp.einsum("kia,lia->kl", trial_vectors, sigmas, precision=lax.Precision.HIGHEST)
    metric = jnp.einsum(
        "kia,lia->kl", trial_vectors, trial_vectors, precision=lax.Precision.HIGHEST
    )
    projected, metric = lax.psum((projected, metric), ("tgt", "src"))
    factor = jnp.linalg.cholesky(metric)
    mixing = jax.scipy.linalg.cho_solve((factor, True), projected)
    residual = sigmas - jnp.einsum(
        "kia,kl->lia", trial_vectors, mixing, precision=lax.Precision.HIGHEST
    )
    totals = lax.psum(jnp.sum(residual * residual, axis=(1, 2)), ("tgt", "src"))
    residual_norms = jnp.sqrt(totals / jnp.diagonal(metric))
    return (sigmas, residual, residual_norms)


def solution(mesh):
    return jax.shard_map(
        shards,
        mesh=mesh,
        in_specs=(
            P(None, ("tgt", "src"), None),
            P("tgt", "src", None, None),
            P("tgt", "src"),
            P("tgt", "src"),
            P(("tgt", "src"), None),
        ),
        out_specs=(P(None, ("tgt", "src"), None), P(None, ("tgt", "src"), None), P()),
        check_vma=False,
    )
```

profile of v0, /device:TPU:1, one launch (start us, length us, event | category | flops | bytes accessed | tf_op | source)
XLA Modules:
  0.0 426.1 jit_solution(354054393823887110)
XLA Ops:
  7.2 40.4 %all_gather.3 = f32[8,32,128]{2,0,1:T(8,128)S(1)} all-gather(f32[8,1,128]{2,0,1:T(8,128)} %bitcast.53), channel_id=1, replica_groups=mesh['tgt'=16,'src'=32] {'src'}, dimensions={1}, use_global_device_ids=true | all-gather | bytes 135168 | tf_op jit(solution)/shard_map/all_gather | solution.py:23
  47.7 13.7 %collective-permute-start = (f32[8,32,128]{2,0,1:T(8,128)S(1)}, f32[8,32,128]{2,0,1:T(8,128)S(1)}, u32[]{:S(2)}, u32[]{:S(2)}) collective-permute-start(f32[8,32,128]{2,0,1:T(8,128)S(1)} %all_gather.3), channel_id=1, source_target_pairs={{0,32},{32,64},{64,96},{96,128},{128,160},{160,192},{192,224},{224... | collective-permute-start | bytes 393224 | tf_op jit(solution)/shard_map/ppermute | solution.py:12
  61.4 1.9 collective-permute-start.1
  63.3 0.7 convert_bitcast_fusion
  64.0 0.7 and_bitcast_fusion
  64.6 3.0 collective-permute-done.1
  67.7 0.6 gather_fusion
  68.3 4.1 fusion.2
  72.4 0.1 fusion.20
  72.5 1.3 dynamic-slice
  73.8 144.4 %all-reduce.4.cloned.1.call-done = f32[8,32,128]{2,0,1:T(8,128)} async-done(((f32[8,32,128]{2,0,1:T(8,128)}), f32[8,32,128]{2,0,1:T(8,128)}) %all-reduce.4.cloned.1.call-update) | async-done | bytes 131088
  218.2 1.3 dynamic-slice_add_fusion
  219.5 0.1 convolution_bitcast_fusion.1
  219.7 100.2 %all-reduce.1 = (f32[8,8]{0,1:T(8,128)S(1)}, f32[8,8]{0,1:T(8,128)S(1)}) all-reduce(f32[8,8]{0,1:T(8,128)S(1)} %convolution_bitcast_fusion.1, f32[8,8]{0,1:T(8,128)S(1)} %fusion.20), channel_id=1, replica_groups=mesh['tgt'=16,'src'=32] {'tgt','src'}, use_global_device_ids=true, to_apply=%region_4.5 | all-reduce | flops 128 | bytes 1024 | tf_op jit(solution)/shard_map/psum | solution.py:43
  319.9 0.7 cholesky.16
  320.7 0.6 compare_reduce_fusion
  321.3 0.6 fusion.12
  322.0 0.6 custom-call.10
  322.6 0.2 fusion.13
  322.8 0.1 fusion.15
  323.0 0.9 multiply_reduce_fusion
  323.9 94.2 %psum.23 = f32[8]{0:T(128)S(1)} all-reduce(f32[8]{0:T(128)S(1)} %get-tuple-element.16), channel_id=1, replica_groups=mesh['tgt'=16,'src'=32] {'tgt','src'}, use_global_device_ids=true, to_apply=%region_6.7 | all-reduce | flops 8 | bytes 64 | tf_op jit(solution)/shard_map/psum | solution.py:49
  418.1 0.6 gather_fusion.1
  418.7 0.5 divide_sqrt_fusion
  (17 shorter events, 0.2 us)
Async XLA Ops:
  7.2 61.1 %copy-start = (f32[32,1,128,128]{3,2,1,0:T(8,128)S(1)}, f32[32,1,128,128]{3,2,1,0:T(8,128)}, u32[]{:S(2)}) copy-start(f32[32,1,128,128]{3,2,1,0:T(8,128)} %param.6) | copy-start | bytes 6291460
  7.2 65.2 %copy-start.1 = (f32[8,1,128]{2,1,0:T(1,128)S(1)}, f32[8,1,128]{2,1,0:T(1,128)}, u32[]{:S(2)}) copy-start(f32[8,1,128]{2,1,0:T(1,128)} %param.5) | copy-start | bytes 12292
  7.2 211.0 %copy-start.3 = (f32[1,128]{1,0:T(1,128)S(1)}, f32[1,128]{1,0:T(1,128)}, u32[]{:S(2)}) copy-start(f32[1,128]{1,0:T(1,128)} %param.9) | copy-start | bytes 1540
  7.2 211.0 %all-reduce.4.cloned.1.call-start = ((), (), s32[]{:S(2)}) async-start(), calls=%async_computation | async-start | bytes 262144
  47.7 17.0 %collective-permute-start = (f32[8,32,128]{2,0,1:T(8,128)S(1)}, f32[8,32,128]{2,0,1:T(8,128)S(1)}, u32[]{:S(2)}, u32[]{:S(2)}) collective-permute-start(f32[8,32,128]{2,0,1:T(8,128)S(1)} %all_gather.3), channel_id=1, source_target_pairs={{0,32},{32,64},{64,96},{96,128},{128,160},{160,192},{192,224},{224... | collective-permute-start | bytes 393224 | tf_op jit(solution)/shard_map/ppermute | solution.py:12
  61.4 6.3 %collective-permute-start.1 = (f32[8,32,128]{2,0,1:T(8,128)S(1)}, f32[8,32,128]{2,0,1:T(8,128)S(1)}, u32[]{:S(2)}, u32[]{:S(2)}) collective-permute-start(f32[8,32,128]{2,0,1:T(8,128)S(1)} %all_gather.3), channel_id=1, source_target_pairs={{32,0},{64,32},{96,64},{128,96},{160,128},{192,160},{224,192},{256... | collective-permute-start | bytes 393224 | tf_op jit(solution)/shard_map/ppermute | solution.py:15
  219.5 199.7 %copy-start.2 = (f32[8,1,128]{2,0,1:T(8,128)}, f32[8,1,128]{2,0,1:T(8,128)S(1)}, u32[]{:S(2)}) copy-start(f32[8,1,128]{2,0,1:T(8,128)S(1)} %dynamic-slice_add_fusion) | copy-start | bytes 12292
Sparse Core Ops, SparseCore 0:
  72.5 145.6 all-reduce.3
where the time goes:
time: 427 us; the launch traced here: 426 us
  blocking collectives  235 us (55%)
  waiting for transfers between devices  147 us (34%)
  starting transfers between devices  15.7 us (4%)
  between operations  14.1 us (3%)
  other arithmetic  5.9 us (1%)
  matrix products  5.55 us (1%)
    unnamed x2, waiting for transfers between devices  144 us
    psum x1, blocking collectives, shards(): projected, metric = lax.psum((projected, metric), ('tgt', 'src'))  100 us
    psum x1, blocking collectives, shards(): totals = lax.psum(jnp.sum(residual * residual, axis=(1, 2)), ('tgt', 'src'))  94.2 us
    all_gather x1, blocking collectives, shards(): source_block = lax.all_gather(trial_vectors, 'src', axis=1, tiled=True)  40.4 us
    ppermute x1, starting transfers between devices, with_halo(): lax.ppermute(lax.slice_in_dim(block, block.shape[dim] - width, None, axis...  13.7 us
  transfers between devices with their start and end apart: 3, of which 2 were waited for; matrix products, arithmetic and copies ran while one was open for 1% of the time, Pallas kernels for 0%

commit v1 on v0

v1 whole, which is shorter than its diff:
```python
import functools

import jax
import jax.numpy as jnp
from jax import lax
from jax.experimental import pallas as pl
from jax.experimental.pallas import tpu as pltpu
from jax.sharding import PartitionSpec as P

MESH = pl.DeviceIdType.MESH
F32 = jnp.float32
BF16 = jnp.bfloat16
HIGHEST = lax.Precision.HIGHEST

NZ, NX, NT = 8, 4, 16
NS = NZ * NX
K, S = 8, 128
CHUNK = 8
NT_DIMS = (((1,), (1,)), ((), ()))


def remote(src, dst, send_sem, recv_sem, device):
    return pltpu.make_async_remote_copy(
        src_ref=src,
        dst_ref=dst,
        send_sem=send_sem,
        recv_sem=recv_sem,
        device_id=device,
        device_id_type=MESH,
    )


def drain(ref, sem):
    pltpu.make_async_copy(ref, ref, sem).wait()


def as_row(pairs):
    full = jnp.concatenate([pairs, jnp.zeros_like(pairs)], axis=0)
    return lax.dot_general(
        jnp.ones((8, S), F32), full, NT_DIMS, precision=HIGHEST, preferred_element_type=F32
    )


def as_tile(row):
    return pltpu.roll(jnp.broadcast_to(row, (K, S)), S - K * (K - 1), 1, stride=K, stride_axis=0)


def kernel(
    trial_hbm,
    couplings_hbm,
    neighbours_hbm,
    live_hbm,
    energies_hbm,
    sigma_ref,
    residual_ref,
    norms_ref,
    own,
    energy,
    raw,
    halves,
    index,
    live,
    rows,
    parts,
    sums,
    row_p,
    row_g,
    row_q,
    row_r,
    row_s,
    tgt_p,
    plane_p,
    tgt_g,
    plane_r,
    tgt_r,
    load_sem,
    chunk_sem,
    z_send,
    z_recv,
    x_send,
    x_recv,
    part_send,
    part_recv,
    small_send,
    small_recv,
):
    t, s = lax.axis_index("tgt"), lax.axis_index("src")
    z, x = s // NX, s % NX

    loads = [
        pltpu.make_async_copy(trial_hbm, own, load_sem.at[0]),
        pltpu.make_async_copy(energies_hbm, energy, load_sem.at[1]),
        pltpu.make_async_copy(neighbours_hbm, index, load_sem.at[2]),
        pltpu.make_async_copy(live_hbm, live, load_sem.at[3]),
    ]
    for load in loads:
        load.start()
    fetches = [
        pltpu.make_async_copy(
            couplings_hbm.at[pl.ds(c * CHUNK, CHUNK)], raw.at[pl.ds(c * CHUNK, CHUNK)], chunk_sem.at[c]
        )
        for c in range(NS // CHUNK)
    ]
    for fetch in fetches:
        fetch.start()

    barrier = pltpu.get_barrier_semaphore()

    def greet(device):
        pl.semaphore_signal(barrier, inc=1, device_id=device, device_id_type=MESH)

    def greet_z(d, _):
        greet((t, ((z + d) % NZ) * NX + x))

    def greet_x(d, _):
        greet((t, z * NX + (x + d) % NX))

    def greet_t(d, _):
        greet(((t + d) % NT, s))

    def greet_halo(j, _):
        greet(((t + 1 + (NT - 2) * (j // 4)) % NT, j * NX + x))

    lax.fori_loop(0, NZ, greet_halo, None)
    lax.fori_loop(1, NZ, greet_z, None)
    lax.fori_loop(1, NT, greet_t, None)
    lax.fori_loop(1, NX, greet_x, None)

    def split(i, _):
        tile = raw[i]
        high = tile.astype(BF16)
        halves[i, :, 0:S] = high
        halves[i, :, S : 2 * S] = (tile - high.astype(F32)).astype(BF16)

    for c, fetch in enumerate(fetches):
        fetch.wait()
        lax.fori_loop(c * CHUNK, (c + 1) * CHUNK, split, None, unroll=2)

    for load in loads:
        load.wait()
    pl.semaphore_wait(barrier, 2 * NZ - 1 + NX - 1 + NT - 1)

    block, other = (t % 2) * NS, (1 - t % 2) * NS
    mine = block + s
    next_t = (t + NT - 1 + 2 * (z // 4)) % NT

    def send_z(d, _):
        to = ((z + d) % NZ) * NX + x
        remote(own, rows.at[mine], z_send.at[0], z_recv.at[z], (t, to)).start()

    def send_halo(d, _):
        to = ((z + d) % NZ) * NX + x
        remote(own, rows.at[mine], z_send.at[0], z_recv.at[NZ + z], (next_t, to)).start()

    def forward(src, at):
        def send_x(d, _):
            to = z * NX + (x + d) % NX
            remote(src, rows.at[at], x_send.at[0], x_recv.at[0], (t, to)).start()

        lax.fori_loop(1, NX, send_x, None)

    lax.fori_loop(0, NZ, send_halo, None)
    lax.fori_loop(1, NZ, send_z, None)
    here = pltpu.make_async_copy(own, rows.at[mine], load_sem.at[0])
    here.start()
    forward(own, mine)
    for d in (1, 7, 2, 6, 3, 5, 4):
        j = (z + d) % NZ
        at = block + j * NX + x
        drain(rows.at[at], z_recv.at[j])
        forward(rows.at[at], at)
    for d in (0, 1, 7, 2, 6, 3, 5, 4):
        j = (z + d) % NZ
        at = other + j * NX + x
        drain(rows.at[at], z_recv.at[NZ + j])
        forward(rows.at[at], at)
    here.wait()
    drain(rows.at[pl.ds(0, 48)], x_recv.at[0])

    def share(i, pairs):
        found = rows[index[0, i] % 64] * live[0, i].astype(F32)
        high = found.astype(BF16).astype(F32)
        low = found - high
        left = jnp.concatenate(
            [jnp.concatenate([high, low], 0), jnp.concatenate([high, jnp.zeros_like(high)], 0)], 1
        ).astype(BF16)
        both = lax.dot_general(left, halves[i], NT_DIMS, preferred_element_type=F32)
        part = both[0:K] + both[K : 2 * K]
        parts[i] = part
        vector = rows[block + i]
        return tuple(
            pairs[l] + vector * jnp.broadcast_to(part[l : l + 1], (K, S)) for l in range(K)
        )

    zeros = tuple(jnp.zeros((K, S), F32) for _ in range(K))
    pairs = lax.fori_loop(0, NS, share, zeros, unroll=8)
    vector = own[...]
    diagonal = vector * energy[...]
    pairs = [
        pairs[l] + vector * jnp.broadcast_to(diagonal[l : l + 1], (K, S)) for l in range(K)
    ]
    row_p[...] = as_row(jnp.concatenate(pairs[::-1], 0))

    def send_tgt(src, buf, sem):
        def one(d, _):
            remote(
                src.at[pl.ds(0, 1)],
                buf.at[pl.ds(t, 1)],
                small_send.at[sem],
                small_recv.at[sem],
                ((t + d) % NT, s),
            ).start()

        lax.fori_loop(1, NT, one, None)
        buf[pl.ds(t, 1), :] = src[0:1, :]

    def wait_tgt(buf, sem):
        drain(buf.at[pl.ds(0, NT - 1)], small_recv.at[sem])
        return jnp.sum(buf[...], axis=0, keepdims=True)

    def send_plane(src, buf, sem):
        def one(d, _):
            to = ((z + d // NX) % NZ) * NX + (x + d % NX) % NX
            remote(
                src.at[pl.ds(0, 1)],
                buf.at[pl.ds(s, 1)],
                small_send.at[sem],
                small_recv.at[sem],
                (t, to),
            ).start()

        lax.fori_loop(1, NS, one, None)
        buf[pl.ds(s, 1), :] = src[0:1, :]

    def wait_plane(buf, sem):
        drain(buf.at[pl.ds(0, NS - 1)], small_recv.at[sem])
        return jnp.sum(buf[...], axis=0, keepdims=True)

    send_tgt(row_p, tgt_p, 0)

    def send_part(d, _):
        to = ((z + d // NX) % NZ) * NX + (x + d % NX) % NX
        remote(parts.at[to], sums.at[s], part_send.at[0], part_recv.at[0], (t, to)).start()

    lax.fori_loop(1, NS, send_part, None)

    def gram(i, pairs):
        vector = rows[block + i]
        return tuple(
            pairs[l] + vector * jnp.broadcast_to(vector[l : l + 1], (K, S)) for l in range(K)
        )

    pairs = lax.fori_loop(0, NS, gram, zeros, unroll=8)
    row_g[...] = as_row(jnp.concatenate(pairs[::-1], 0))
    send_tgt(row_g, tgt_g, 1)

    row_q[...] = jnp.broadcast_to(wait_tgt(tgt_p, 0), (8, S))
    send_plane(row_q, plane_p, 2)

    metric = as_tile(wait_tgt(tgt_g, 1))
    lane = lax.broadcasted_iota(jnp.int32, (K, S), 1)
    sub = lax.broadcasted_iota(jnp.int32, (K, S), 0)
    norms2 = jnp.sum(jnp.where(lane == sub, metric, 0.0), axis=0, keepdims=True)
    work = metric
    solved = vector
    factors = []
    for j in range(K):
        column = jnp.broadcast_to(work[:, j : j + 1], (K, S))
        pivot = lax.rsqrt(jnp.broadcast_to(column[j : j + 1], (K, S)))
        column = jnp.where(sub >= j, column * pivot, 0.0)
        factors.append((column, pivot))
        line = jnp.sum(jnp.where(lane == sub, column, 0.0), axis=0, keepdims=True)
        work = work - column * jnp.broadcast_to(line, (K, S))
        top = jnp.broadcast_to(solved[j : j + 1], (K, S)) * pivot
        solved = jnp.where(sub == j, top, solved - jnp.where(sub > j, column * top, 0.0))
    for j in reversed(range(K)):
        column, pivot = factors[j]
        dots = jnp.sum(jnp.where(sub > j, column * solved, 0.0), axis=0, keepdims=True)
        value = (solved - jnp.broadcast_to(dots, (K, S))) * pivot
        solved = jnp.where(sub == j, value, solved)

    drain(sums.at[pl.ds(0, NS - 1)], part_recv.at[0])
    sums[s] = parts[s]
    sigma = jnp.sum(sums[...], axis=0) + diagonal
    sigma_ref[...] = sigma

    projected = as_tile(wait_plane(plane_p, 2))
    residual = sigma
    for j in range(K):
        residual = residual - jnp.broadcast_to(projected[:, j : j + 1], (K, S)) * jnp.broadcast_to(
            solved[j : j + 1], (K, S)
        )
    residual_ref[...] = residual
    square = residual * residual
    row_r[...] = lax.dot_general(
        jnp.ones((8, S), F32),
        jnp.concatenate([square, jnp.zeros((S - K, S), F32)], 0),
        NT_DIMS,
        precision=HIGHEST,
        preferred_element_type=F32,
    )
    send_plane(row_r, plane_r, 3)
    row_s[...] = jnp.broadcast_to(wait_plane(plane_r, 3), (8, S))
    send_tgt(row_s, tgt_r, 4)
    total = wait_tgt(tgt_r, 4)
    norms_ref[...] = jnp.sqrt(total / jnp.where(lane[0:1] < K, norms2, 1.0))

    drain(rows.at[pl.ds(0, 2 * NZ - 1)], z_send.at[0])
    drain(rows.at[pl.ds(0, 48)], x_send.at[0])
    drain(parts.at[pl.ds(0, NS - 1)], part_send.at[0])
    for sem, buf, count in ((0, tgt_p, NT), (1, tgt_g, NT), (2, plane_p, NS), (3, plane_r, NS), (4, tgt_r, NT)):
        drain(buf.at[pl.ds(0, count - 1)], small_send.at[sem])


def shards(trial_vectors, couplings, neighbours, live_slots, energies):
    hbm = pl.BlockSpec(memory_space=pltpu.HBM)
    vmem = pl.BlockSpec(memory_space=pltpu.VMEM)
    dma = pltpu.SemaphoreType.DMA
    sigma, residual, norms = pl.pallas_call(
        kernel,
        out_shape=(
            jax.ShapeDtypeStruct((K, S), F32),
            jax.ShapeDtypeStruct((K, S), F32),
            jax.ShapeDtypeStruct((1, S), F32),
        ),
        in_specs=[hbm] * 5,
        out_specs=(vmem, vmem, vmem),
        scratch_shapes=[
            pltpu.VMEM((K, S), F32),
            pltpu.VMEM((1, S), F32),
            pltpu.VMEM((NS, S, S), F32),
            pltpu.VMEM((NS, S, 2 * S), BF16),
            pltpu.SMEM((1, NS), jnp.int32),
            pltpu.SMEM((1, NS), jnp.int32),
            pltpu.VMEM((64, K, S), F32),
            pltpu.VMEM((NS, K, S), F32),
            pltpu.VMEM((NS, K, S), F32),
            pltpu.VMEM((8, S), F32),
            pltpu.VMEM((8, S), F32),
            pltpu.VMEM((8, S), F32),
            pltpu.VMEM((8, S), F32),
            pltpu.VMEM((8, S), F32),
            pltpu.VMEM((NT, S), F32),
            pltpu.VMEM((NS, S), F32),
            pltpu.VMEM((NT, S), F32),
            pltpu.VMEM((NS, S), F32),
            pltpu.VMEM((NT, S), F32),
            dma((4,)),
            dma((NS // CHUNK,)),
            dma((1,)),
            dma((2 * NZ,)),
            dma((1,)),
            dma((1,)),
            dma((1,)),
            dma((1,)),
            dma((5,)),
            dma((5,)),
        ],
        compiler_params=pltpu.CompilerParams(collective_id=0, has_side_effects=True),
        name="davidson",
    )(
        trial_vectors.reshape(K, S),
        couplings.reshape(NS, S, S),
        neighbours.reshape(1, NS),
        live_slots.reshape(1, NS),
        energies,
    )
    return sigma.reshape(K, 1, S), residual.reshape(K, 1, S), norms[0, :K]


def solution(mesh):
    return jax.shard_map(
        shards,
        mesh=mesh,
        in_specs=(
            P(None, ("tgt", "src"), None),
            P("tgt", "src", None, None),
            P("tgt", "src"),
            P("tgt", "src"),
            P(("tgt", "src"), None),
        ),
        out_specs=(P(None, ("tgt", "src"), None), P(None, ("tgt", "src"), None), P()),
        check_vma=False,
    )
```

time: 427 us -> 52.8 us (0.12)
  blocking collectives: 235 us -> 0 us
  waiting for transfers between devices: 147 us -> 0 us
  Pallas kernels: 0 us -> 48.2 us
  starting transfers between devices: 15.7 us -> 0 us
  between operations: 14.1 us -> 0.64 us
  other arithmetic: 5.9 us -> 0 us
  matrix products: 5.55 us -> 0 us
    psum x2 -> x0, blocking collectives: 194 us -> none  [the longest x1 100 us: shards(): projected, metric = lax.psum((projected, metric), ('tgt', 'src'))]
    unnamed x2 -> x0, waiting for transfers between devices: 144 us -> none
    pallas_call x0 -> x1, Pallas kernels: none -> 48.2 us  [shards(): pl.pallas_call(kernel, out_shape=(jax.ShapeDtypeStruct((K, S), F32), jax....]
    all_gather x1 -> x0, blocking collectives: 40.4 us -> none  [shards(): source_block = lax.all_gather(trial_vectors, 'src', axis=1, tiled=True)]
    ppermute x2 -> x0, starting transfers between devices: 15.6 us -> none  [the longest x1 13.7 us: with_halo(): lax.ppermute(lax.slice_in_dim(block, block.shape[dim] - width, None, axis...]
    dot_general x4 -> x0, matrix products: 5.22 us -> none  [the longest x1 4.05 us: shards(): jnp.einsum('inab,kinb->kia', couplings, fetched, precision=lax.Precision....]
  transfers between devices with their start and end apart: 3 -> 0, of which waited for: 2 -> 0; matrix products, arithmetic and copies ran while one was open for 1% -> 0% of each run, Pallas kernels for 0% -> 0%
where the time goes in v1:
time: 52.8 us; the launch traced here: 52.6 us
  Pallas kernels  48.2 us (91%)
  local copies, waits for them, and re-layouts  3.7 us (7%)
  between operations  0.64 us (1%)
    pallas_call x1, Pallas kernels, shards(): pl.pallas_call(kernel, out_shape=(jax.ShapeDtypeStruct((K, S), F32), jax....  48.2 us
    unnamed x2, local copies, waits for them, and re-layouts  2.53 us
    squeeze x1, local copies, waits for them, and re-layouts, shards(): return (sigma.reshape(K, 1, S), residual.reshape(K, 1, S), norms[0, :K])  1.18 us

profile of v1, /device:TPU:1, one launch (start us, length us, event | category | flops | bytes accessed | tf_op | source)
XLA Modules:
  0.0 52.6 jit_solution(18389026571291635746)
XLA Ops:
  0.6 48.2 %davidson.1 = (f32[8,128]{1,0:T(8,128)}, f32[8,128]{1,0:T(8,128)}, f32[1,128]{1,0:T(1,128)}) custom-call(f32[8,128]{1,0:T(8,128)} %bitcast.13, f32[32,128,128]{2,1,0:T(8,128)} %bitcast.12, s32[1,32]{1,0:T(1,128)} %bitcast.16, s32[1,32]{1,0:T(1,128)} %bitcast.17, f32[1,128]{1,0:T(1,128)} %energies_hbm.1), custom_call_target="tpu_custom_call" | custom-call | tf_op jit(solution)/shard_map/davidson/pallas_call | solution.py:319
  48.9 1.2 %slice_bitcast_fusion = f32[8]{0:T(128)} fusion(f32[1,128]{1,0:T(1,128)} %get-tuple-element.8), kind=kLoop, calls=%fused_computation | loop fusion | bytes 64 | tf_op jit(solution)/shard_map/squeeze | solution.py:368
  50.1 1.3 %copy.12 = f32[8,1,128]{2,1,0:T(1,128)} copy(f32[8,1,128]{2,1,0:T(1,128)} %bitcast.15) | data formatting | bytes 8192
  51.3 1.3 %copy.13 = f32[8,1,128]{2,1,0:T(1,128)} copy(f32[8,1,128]{2,1,0:T(1,128)} %bitcast.14) | data formatting | bytes 8192

commit v2 on v1

--- a/solution.py
+++ b/solution.py
@@ -51,9 +51,7 @@
     neighbours_hbm,
     live_hbm,
     energies_hbm,
-    sigma_ref,
-    residual_ref,
-    norms_ref,
+    packed_ref,
     own,
     energy,
     raw,
@@ -75,10 +73,16 @@
     tgt_r,
     load_sem,
     chunk_sem,
-    z_send,
-    z_recv,
+    in_z,
+    in_x,
+    in_t,
+    up_send,
+    up_recv,
+    halo_recv,
     x_send,
     x_recv,
+    bulk_send,
+    bulk_recv,
     part_send,
     part_recv,
     small_send,
@@ -105,26 +109,60 @@
         fetch.start()
 
     barrier = pltpu.get_barrier_semaphore()
-
-    def greet(device):
-        pl.semaphore_signal(barrier, inc=1, device_id=device, device_id_type=MESH)
-
-    def greet_z(d, _):
-        greet((t, ((z + d) % NZ) * NX + x))
-
-    def greet_x(d, _):
-        greet((t, z * NX + (x + d) % NX))
-
-    def greet_t(d, _):
-        greet(((t + d) % NT, s))
-
-    def greet_halo(j, _):
-        greet(((t + 1 + (NT - 2) * (j // 4)) % NT, j * NX + x))
-
-    lax.fori_loop(0, NZ, greet_halo, None)
-    lax.fori_loop(1, NZ, greet_z, None)
-    lax.fori_loop(1, NT, greet_t, None)
-    lax.fori_loop(1, NX, greet_x, None)
+    halo_t = (t + NT - 1 + 2 * (z // 4)) % NT
+
+    def signal(sem, device):
+        pl.semaphore_signal(sem, inc=1, device_id=device, device_id_type=MESH)
+
+    def greet_z(j, _):
+        signal(barrier, (t, j * NX + x))
+        signal(barrier, ((t + 1 + (NT - 2) * (j // 4)) % NT, j * NX + x))
+
+    lax.fori_loop(z + 1, NZ, greet_z, None)
+    lax.fori_loop(x + 1, NX, lambda j, _: signal(barrier, (t, z * NX + j)), None)
+    lax.fori_loop(t + 1, NT, lambda j, _: signal(barrier, (j, s)), None)
+    before = 2 * z + x + t
+
+    @pl.when(before > 0)
+    def _():
+        pl.semaphore_wait(barrier, before)
+
+    lax.fori_loop(0, z, lambda j, _: signal(in_z.at[z], (t, j * NX + x)), None)
+    lax.fori_loop(0, x, lambda j, _: signal(in_x.at[x], (t, z * NX + j)), None)
+    lax.fori_loop(0, t, lambda j, _: signal(in_t.at[t], (j, s)), None)
+
+    block, other = (t % 2) * NS, (1 - t % 2) * NS
+    mine = block + s
+
+    loads[0].wait()
+
+    def send_up(j, _):
+        to = j * NX + x
+        remote(own, rows.at[mine], up_send.at[j], halo_recv.at[z], (halo_t, to)).start()
+        remote(own, rows.at[mine], up_send.at[j], up_recv.at[z], (t, to)).start()
+
+    lax.fori_loop(0, z, send_up, None)
+    here = pltpu.make_async_copy(own, rows.at[mine], load_sem.at[0])
+    here.start()
+
+    @pl.when(halo_t > t)
+    def _():
+        pl.semaphore_wait(in_t.at[halo_t], 1)
+
+    remote(own, rows.at[mine], up_send.at[z], halo_recv.at[z], (halo_t, s)).start()
+
+    def forward(src, at, j):
+        def send_x(d, _):
+            to = z * NX + (x + d) % NX
+            remote(src, rows.at[at], x_send.at[j], x_recv.at[j], (t, to)).start()
+
+        lax.fori_loop(1, NX, send_x, None)
+
+    lax.fori_loop(x + 1, NX, lambda j, _: pl.semaphore_wait(in_x.at[j], 1), None)
+    forward(own, mine, z)
+    beside = other + s
+    drain(rows.at[beside], halo_recv.at[z])
+    forward(rows.at[beside], beside, z)
 
     def split(i, _):
         tile = raw[i]
@@ -135,47 +173,26 @@
     for c, fetch in enumerate(fetches):
         fetch.wait()
         lax.fori_loop(c * CHUNK, (c + 1) * CHUNK, split, None, unroll=2)
-
-    for load in loads:
+    for load in loads[1:]:
         load.wait()
-    pl.semaphore_wait(barrier, 2 * NZ - 1 + NX - 1 + NT - 1)
-
-    block, other = (t % 2) * NS, (1 - t % 2) * NS
-    mine = block + s
-    next_t = (t + NT - 1 + 2 * (z // 4)) % NT
-
-    def send_z(d, _):
-        to = ((z + d) % NZ) * NX + x
-        remote(own, rows.at[mine], z_send.at[0], z_recv.at[z], (t, to)).start()
-
-    def send_halo(d, _):
-        to = ((z + d) % NZ) * NX + x
-        remote(own, rows.at[mine], z_send.at[0], z_recv.at[NZ + z], (next_t, to)).start()
-
-    def forward(src, at):
-        def send_x(d, _):
-            to = z * NX + (x + d) % NX
-            remote(src, rows.at[at], x_send.at[0], x_recv.at[0], (t, to)).start()
-
-        lax.fori_loop(1, NX, send_x, None)
-
-    lax.fori_loop(0, NZ, send_halo, None)
-    lax.fori_loop(1, NZ, send_z, None)
-    here = pltpu.make_async_copy(own, rows.at[mine], load_sem.at[0])
-    here.start()
-    forward(own, mine)
-    for d in (1, 7, 2, 6, 3, 5, 4):
-        j = (z + d) % NZ
+    here.wait()
+    drain(rows.at[pl.ds(0, 6)], x_recv.at[z])
+
+    def after(j, _):
+        pl.semaphore_wait(in_z.at[j], 1)
+        for side in (block, other):
+            four = rows.at[pl.ds(side + z * NX, NX)]
+            remote(four, four, bulk_send.at[j], bulk_recv.at[z], (t, j * NX + x)).start()
         at = block + j * NX + x
-        drain(rows.at[at], z_recv.at[j])
-        forward(rows.at[at], at)
-    for d in (0, 1, 7, 2, 6, 3, 5, 4):
-        j = (z + d) % NZ
+        drain(rows.at[at], up_recv.at[j])
+        forward(rows.at[at], at, j)
         at = other + j * NX + x
-        drain(rows.at[at], z_recv.at[NZ + j])
-        forward(rows.at[at], at)
-    here.wait()
-    drain(rows.at[pl.ds(0, 48)], x_recv.at[0])
+        drain(rows.at[at], halo_recv.at[j])
+        forward(rows.at[at], at, j)
+
+    lax.fori_loop(z + 1, NZ, after, None)
+    lax.fori_loop(0, z, lambda j, _: drain(rows.at[pl.ds(0, 2 * NX)], bulk_recv.at[j]), None)
+    lax.fori_loop(z + 1, NZ, lambda j, _: drain(rows.at[pl.ds(0, 6)], x_recv.at[j]), None)
 
     def share(i, pairs):
         found = rows[index[0, i] % 64] * live[0, i].astype(F32)
@@ -236,6 +253,12 @@
         drain(buf.at[pl.ds(0, NS - 1)], small_recv.at[sem])
         return jnp.sum(buf[...], axis=0, keepdims=True)
 
+    def wait_in(j, _):
+        @pl.when(j != halo_t)
+        def _():
+            pl.semaphore_wait(in_t.at[j], 1)
+
+    lax.fori_loop(t + 1, NT, wait_in, None)
     send_tgt(row_p, tgt_p, 0)
 
     def send_part(d, _):
@@ -282,7 +305,8 @@
     drain(sums.at[pl.ds(0, NS - 1)], part_recv.at[0])
     sums[s] = parts[s]
     sigma = jnp.sum(sums[...], axis=0) + diagonal
-    sigma_ref[...] = sigma
+    packed_ref[2 * K : 3 * K] = jnp.zeros((K, S), F32)
+    packed_ref[0:K] = sigma
 
     projected = as_tile(wait_plane(plane_p, 2))
     residual = sigma
@@ -290,7 +314,7 @@
         residual = residual - jnp.broadcast_to(projected[:, j : j + 1], (K, S)) * jnp.broadcast_to(
             solved[j : j + 1], (K, S)
         )
-    residual_ref[...] = residual
+    packed_ref[K : 2 * K] = residual
     square = residual * residual
     row_r[...] = lax.dot_general(
         jnp.ones((8, S), F32),
@@ -303,28 +327,35 @@
     row_s[...] = jnp.broadcast_to(wait_plane(plane_r, 3), (8, S))
     send_tgt(row_s, tgt_r, 4)
     total = wait_tgt(tgt_r, 4)
-    norms_ref[...] = jnp.sqrt(total / jnp.where(lane[0:1] < K, norms2, 1.0))
-
-    drain(rows.at[pl.ds(0, 2 * NZ - 1)], z_send.at[0])
-    drain(rows.at[pl.ds(0, 48)], x_send.at[0])
+    packed_ref[2 * K : 2 * K + 1] = jnp.sqrt(total / jnp.where(lane[0:1] < K, norms2, 1.0))
+
+    lax.fori_loop(0, z, lambda j, _: drain(rows.at[pl.ds(0, 2)], up_send.at[j]), None)
+    drain(rows.at[0], up_send.at[z])
+    lax.fori_loop(z, NZ, lambda j, _: drain(rows.at[pl.ds(0, 6)], x_send.at[j]), None)
+    lax.fori_loop(
+        z + 1, NZ, lambda j, _: drain(rows.at[pl.ds(0, 2 * NX)], bulk_send.at[j]), None
+    )
     drain(parts.at[pl.ds(0, NS - 1)], part_send.at[0])
     for sem, buf, count in ((0, tgt_p, NT), (1, tgt_g, NT), (2, plane_p, NS), (3, plane_r, NS), (4, tgt_r, NT)):
         drain(buf.at[pl.ds(0, count - 1)], small_send.at[sem])
+
+
+def finish(packed_ref, sigma_ref, residual_ref, norms_ref):
+    sigma_ref[...] = packed_ref[0:K]
+    residual_ref[...] = packed_ref[K : 2 * K]
+    norms_ref[...] = packed_ref[2 * K : 2 * K + 1, 0:K]
 
 
 def shards(trial_vectors, couplings, neighbours, live_slots, energies):
     hbm = pl.BlockSpec(memory_space=pltpu.HBM)
     vmem = pl.BlockSpec(memory_space=pltpu.VMEM)
     dma = pltpu.SemaphoreType.DMA
-    sigma, residual, norms = pl.pallas_call(
+    regular = pltpu.SemaphoreType.REGULAR
+    packed = pl.pallas_call(
         kernel,
-        out_shape=(
-            jax.ShapeDtypeStruct((K, S), F32),
-            jax.ShapeDtypeStruct((K, S), F32),
-            jax.ShapeDtypeStruct((1, S), F32),
-        ),
+        out_shape=jax.ShapeDtypeStruct((3 * K, S), F32),
         in_specs=[hbm] * 5,
-        out_specs=(vmem, vmem, vmem),
+        out_specs=vmem,
         scratch_shapes=[
             pltpu.VMEM((K, S), F32),
             pltpu.VMEM((1, S), F32),
@@ -347,10 +378,16 @@
             pltpu.VMEM((NT, S), F32),
             dma((4,)),
             dma((NS // CHUNK,)),
-            dma((1,)),
-            dma((2 * NZ,)),
-            dma((1,)),
-            dma((1,)),
+            regular((NZ,)),
+            regular((NX,)),
+            regular((NT,)),
+            dma((NZ,)),
+            dma((NZ,)),
+            dma((NZ,)),
+            dma((NZ,)),
+            dma((NZ,)),
+            dma((NZ,)),
+            dma((NZ,)),
             dma((1,)),
             dma((1,)),
             dma((5,)),
@@ -365,7 +402,18 @@
         live_slots.reshape(1, NS),
         energies,
     )
-    return sigma.reshape(K, 1, S), residual.reshape(K, 1, S), norms[0, :K]
+    sigma, residual, norms = pl.pallas_call(
+        finish,
+        out_shape=(
+            jax.ShapeDtypeStruct((K, S), F32),
+            jax.ShapeDtypeStruct((K, S), F32),
+            jax.ShapeDtypeStruct((1, K), F32),
+        ),
+        in_specs=[vmem],
+        out_specs=(vmem, vmem, vmem),
+        name="finish",
+    )(packed)
+    return sigma.reshape(K, 1, S), residual.reshape(K, 1, S), norms.reshape(K)
 
 
 def solution(mesh):

time: 52.8 us -> 51.6 us (0.977)
  local copies, waits for them, and re-layouts: 3.7 us -> 0 us
  Pallas kernels: 48.2 us -> 50.7 us
    unnamed x2 -> x0, local copies, waits for them, and re-layouts: 2.53 us -> none
    pallas_call x1 -> x2, Pallas kernels: 48.2 us -> 50.7 us  [the longest x1 49.4 us: shards(): pl.pallas_call(kernel, out_shape=jax.ShapeDtypeStruct((3 * K, S), F32), i...]
    squeeze x1 -> x0, local copies, waits for them, and re-layouts: 1.18 us -> none  [shards(): return (sigma.reshape(K, 1, S), residual.reshape(K, 1, S), norms[0, :K])]
where the time goes in v2:
time: 51.6 us; the launch traced here: 51.4 us
  Pallas kernels  50.7 us (98%)
  between operations  0.64 us (1%)
    pallas_call x1, Pallas kernels, shards(): pl.pallas_call(kernel, out_shape=jax.ShapeDtypeStruct((3 * K, S), F32), i...  49.4 us
    pallas_call x1, Pallas kernels, shards(): pl.pallas_call(finish, out_shape=(jax.ShapeDtypeStruct((K, S), F32), jax....  1.31 us

profile of v2, /device:TPU:1, one launch (start us, length us, event | category | flops | bytes accessed | tf_op | source)
XLA Modules:
  0.0 51.4 jit_solution(13782840151669603574)
XLA Ops:
  0.6 49.4 %davidson.1.packed_ref = f32[24,128]{1,0:T(8,128)} custom-call(f32[8,128]{1,0:T(8,128)} %bitcast.12, f32[32,128,128]{2,1,0:T(8,128)} %bitcast.11, s32[1,32]{1,0:T(1,128)} %bitcast.13, s32[1,32]{1,0:T(1,128)} %bitcast.14, f32[1,128]{1,0:T(1,128)} %energies_hbm.1), custom_call_target="tpu_custom_call" | custom-call | tf_op jit(solution)/shard_map/davidson/pallas_call | solution.py:354
  50.1 1.3 %finish.1 = (f32[8,128]{1,0:T(8,128)}, f32[8,128]{1,0:T(8,128)}, f32[1,8]{1,0:T(1,128)}) custom-call(f32[24,128]{1,0:T(8,128)} %davidson.1.packed_ref), custom_call_target="tpu_custom_call" | custom-call | tf_op jit(solution)/shard_map/finish/pallas_call | solution.py:405

commit v3 on v2

v3 whole, which is shorter than its diff:
```python
import functools

import jax
import jax.numpy as jnp
from jax import lax
from jax.experimental import pallas as pl
from jax.experimental.pallas import tpu as pltpu
from jax.sharding import PartitionSpec as P

MESH = pl.DeviceIdType.MESH
F32 = jnp.float32
BF16 = jnp.bfloat16
HIGHEST = lax.Precision.HIGHEST

NZ, NX, NT = 8, 4, 16
NS = NZ * NX
K, S = 8, 128
SHIFT = 2.0
CHUNK = 8
NT_DIMS = (((1,), (1,)), ((), ()))


def remote(src, dst, send_sem, recv_sem, device):
    return pltpu.make_async_remote_copy(
        src_ref=src,
        dst_ref=dst,
        send_sem=send_sem,
        recv_sem=recv_sem,
        device_id=device,
        device_id_type=MESH,
    )


def drain(ref, sem):
    pltpu.make_async_copy(ref, ref, sem).wait()


def as_row(pairs):
    full = jnp.concatenate([pairs, jnp.zeros_like(pairs)], axis=0)
    return lax.dot_general(
        jnp.ones((8, S), F32), full, NT_DIMS, precision=HIGHEST, preferred_element_type=F32
    )


def as_row8(tile):
    full = jnp.concatenate([tile, jnp.zeros((S - K, S), F32)], axis=0)
    return lax.dot_general(
        jnp.ones((8, S), F32), full, NT_DIMS, precision=HIGHEST, preferred_element_type=F32
    )


def as_tile(row):
    return pltpu.roll(jnp.broadcast_to(row, (K, S)), S - K * (K - 1), 1, stride=K, stride_axis=0)


def kernel(
    trial_hbm,
    couplings_hbm,
    neighbours_hbm,
    live_hbm,
    energies_hbm,
    packed_ref,
    own,
    energy,
    raw,
    halves,
    index,
    live,
    rows,
    parts,
    sums,
    row_p,
    row_g,
    row_q,
    row_s,
    row_u,
    tgt_p,
    plane_p,
    tgt_g,
    plane_s,
    tgt_s,
    load_sem,
    chunk_sem,
    z_send,
    z_recv,
    x_send,
    x_recv,
    part_send,
    part_recv,
    small_send,
    small_recv,
):
    t, s = lax.axis_index("tgt"), lax.axis_index("src")
    z, x = s // NX, s % NX

    loads = [
        pltpu.make_async_copy(trial_hbm, own, load_sem.at[0]),
        pltpu.make_async_copy(energies_hbm, energy, load_sem.at[1]),
        pltpu.make_async_copy(neighbours_hbm, index, load_sem.at[2]),
        pltpu.make_async_copy(live_hbm, live, load_sem.at[3]),
    ]
    loads[0].start()

    barrier = pltpu.get_barrier_semaphore()

    def greet(device):
        pl.semaphore_signal(barrier, inc=1, device_id=device, device_id_type=MESH)

    def along_z(d):
        return ((z + d) % NZ) * NX + x

    def along_x(d):
        return z * NX + (x + d) % NX

    def greet_beside(d, _):
        greet(((t + 1) % NT, along_x(d)))
        greet(((t + NT - 1) % NT, along_x(d)))

    lax.fori_loop(1, NZ, lambda d, _: greet((t, along_z(d))), None)
    lax.fori_loop(0, NX, greet_beside, None)
    lax.fori_loop(2, NT - 1, lambda d, _: greet(((t + d) % NT, s)), None)
    lax.fori_loop(1, NX, lambda d, _: greet((t, along_x(d))), None)

    for load in loads[1:]:
        load.start()
    fetches = [
        pltpu.make_async_copy(
            couplings_hbm.at[pl.ds(c * CHUNK, CHUNK)], raw.at[pl.ds(c * CHUNK, CHUNK)], chunk_sem.at[c]
        )
        for c in range(NS // CHUNK)
    ]
    for fetch in fetches:
        fetch.start()
    loads[0].wait()
    pl.semaphore_wait(barrier, NZ - 1 + 2 * NX + NT - 3 + NX - 1)

    block = (t % 2) * NS
    mine = block + s

    def send_z(d, _):
        remote(own, rows.at[mine], z_send.at[0], z_recv.at[z], (t, along_z(d))).start()

    lax.fori_loop(1, NZ, send_z, None)
    here = pltpu.make_async_copy(own, rows.at[mine], load_sem.at[0])
    here.start()

    def forward(src, j):
        at = block + j * NX + x
        beside = (t + NT - 1 + 2 * (j // 4)) % NT

        def send_beside(d, _):
            remote(src, rows.at[at], x_send.at[0], x_recv.at[0], (beside, along_x(d))).start()

        def send_x(d, _):
            remote(src, rows.at[at], x_send.at[0], x_recv.at[0], (t, along_x(d))).start()

        lax.fori_loop(0, NX, send_beside, None)
        lax.fori_loop(1, NX, send_x, None)

    forward(own, z)

    def split(i, _):
        tile = raw[i]
        high = tile.astype(BF16)
        halves[i, :, 0:S] = high
        halves[i, :, S : 2 * S] = (tile - high.astype(F32)).astype(BF16)

    for c, fetch in enumerate(fetches):
        fetch.wait()
        lax.fori_loop(c * CHUNK, (c + 1) * CHUNK, split, None, unroll=2)
    for load in loads[1:]:
        load.wait()
    here.wait()

    for d in (1, 7, 2, 6, 3, 5, 4):
        j = (z + d) % NZ
        row = rows.at[block + j * NX + x]
        drain(row, z_recv.at[j])
        forward(row, j)
    drain(rows.at[pl.ds(0, 2 * NS - NZ)], x_recv.at[0])

    def share(i, _):
        found = rows[index[0, i] % 64] * live[0, i].astype(F32)
        high = found.astype(BF16).astype(F32)
        low = found - high
        left = jnp.concatenate(
            [jnp.concatenate([high, low], 0), jnp.concatenate([high, jnp.zeros_like(high)], 0)], 1
        ).astype(BF16)
        both = lax.dot_general(left, halves[i], NT_DIMS, preferred_element_type=F32)
        parts[i] = both[0:K] + both[K : 2 * K]

    def send_parts(d):
        def send_part(e, _):
            to = ((z + d) % NZ) * NX + (x + e) % NX
            remote(parts.at[to], sums.at[s], part_send.at[0], part_recv.at[0], (t, to)).start()

        lax.fori_loop(0 if d else 1, NX, send_part, None)

    order = (4, 3, 5, 2, 6, 1, 7, 0)
    for n, d in enumerate(order):
        first = ((z + d) % NZ) * NX
        lax.fori_loop(0, NX, lambda e, _: share(first + e, None), None, unroll=True)
        if n:
            send_parts(order[n - 1])

    def outer(pairs, left, right):
        return tuple(
            pairs[l] + left * jnp.broadcast_to(right[l : l + 1], (K, S)) for l in range(K)
        )

    vector = own[...]
    diagonal = vector * (energy[...] - SHIFT)
    zeros = tuple(jnp.zeros((K, S), F32) for _ in range(K))
    pairs = lax.fori_loop(
        0, NS // 2, lambda i, p: outer(p, rows[block + i], parts[i]), zeros, unroll=8
    )
    send_parts(order[-1])
    pairs = lax.fori_loop(
        NS // 2, NS, lambda i, p: outer(p, rows[block + i], parts[i]), pairs, unroll=8
    )
    pairs = outer(pairs, vector, diagonal)
    row_p[...] = as_row(jnp.concatenate(pairs[::-1], 0))

    def send_tgt(src, buf, sem):
        def one(d, _):
            remote(
                src.at[pl.ds(0, 1)],
                buf.at[pl.ds(t, 1)],
                small_send.at[sem],
                small_recv.at[sem],
                ((t + d) % NT, s),
            ).start()

        lax.fori_loop(1, NT, one, None)
        buf[pl.ds(t, 1), :] = src[0:1, :]

    def wait_tgt(buf, sem):
        drain(buf.at[pl.ds(0, NT - 1)], small_recv.at[sem])
        return jnp.sum(buf[...], axis=0, keepdims=True)

    def send_plane(src, buf, sem):
        def one(d, _):
            to = ((z + 4 + d // NX) % NZ) * NX + (x + 2 + d % NX) % NX

            @pl.when(to != s)
            def _():
                remote(
                    src.at[pl.ds(0, 1)],
                    buf.at[pl.ds(s, 1)],
                    small_send.at[sem],
                    small_recv.at[sem],
                    (t, to),
                ).start()

        lax.fori_loop(0, NS, one, None)
        buf[pl.ds(s, 1), :] = src[0:1, :]

    def wait_plane(buf, sem):
        drain(buf.at[pl.ds(0, NS - 1)], small_recv.at[sem])
        return jnp.sum(buf[...], axis=0, keepdims=True)

    send_tgt(row_p, tgt_p, 0)

    def gram(i, p):
        return outer(p, rows[block + i], rows[block + i])

    pairs = lax.fori_loop(0, NS, gram, zeros, unroll=8)
    row_g[...] = as_row(jnp.concatenate(pairs[::-1], 0))
    send_tgt(row_g, tgt_g, 1)

    drain(sums.at[pl.ds(0, NS - 1)], part_recv.at[0])
    sums[s] = parts[s]
    shifted = jnp.sum(sums[...], axis=0) + diagonal
    row_s[...] = as_row8(shifted * shifted)
    send_plane(row_s, plane_s, 3)
    packed_ref[2 * K : 3 * K] = jnp.zeros((K, S), F32)
    packed_ref[0:K] = shifted + SHIFT * vector

    row_q[...] = jnp.broadcast_to(wait_tgt(tgt_p, 0), (8, S))
    send_plane(row_q, plane_p, 2)

    metric = as_tile(wait_tgt(tgt_g, 1))
    lane = lax.broadcasted_iota(jnp.int32, (K, S), 1)
    sub = lax.broadcasted_iota(jnp.int32, (K, S), 0)
    norms2 = jnp.sum(jnp.where(lane == sub, metric, 0.0), axis=0, keepdims=True)
    work = metric
    solved = [vector, jnp.where(lane == sub, 1.0, 0.0)]
    factors = []
    for j in range(K):
        column = jnp.broadcast_to(work[:, j : j + 1], (K, S))
        pivot = lax.rsqrt(jnp.broadcast_to(column[j : j + 1], (K, S)))
        column = jnp.where(sub >= j, column * pivot, 0.0)
        factors.append((column, pivot))
        line = jnp.sum(jnp.where(lane == sub, column, 0.0), axis=0, keepdims=True)
        work = work - column * jnp.broadcast_to(line, (K, S))
        for n in range(2):
            top = jnp.broadcast_to(solved[n][j : j + 1], (K, S)) * pivot
            below = solved[n] - jnp.where(sub > j, column * top, 0.0)
            solved[n] = jnp.where(sub == j, top, below)
    for j in reversed(range(K)):
        column, pivot = factors[j]
        for n in range(2):
            dots = jnp.sum(jnp.where(sub > j, column * solved[n], 0.0), axis=0, keepdims=True)
            value = (solved[n] - jnp.broadcast_to(dots, (K, S))) * pivot
            solved[n] = jnp.where(sub == j, value, solved[n])
    solved, inverse = solved

    row_u[...] = jnp.broadcast_to(wait_plane(plane_s, 3), (8, S))
    send_tgt(row_u, tgt_s, 4)

    def times(left, right):
        total = jnp.zeros((K, S), F32)
        for j in range(K):
            total = total + jnp.broadcast_to(left[:, j : j + 1], (K, S)) * jnp.broadcast_to(
                right[j : j + 1], (K, S)
            )
        return total

    projected = as_tile(wait_plane(plane_p, 2))
    packed_ref[K : 2 * K] = shifted - times(projected, solved)
    square_mesh = (lane < K) & (sub < K)
    mixing = times(projected, inverse)
    missing = projected - times(mixing, metric)
    taken = as_row8(jnp.where(square_mesh, mixing * (projected + missing), 0.0))

    left_over = jnp.maximum(wait_tgt(tgt_s, 4) - taken[0:1], 0.0)
    packed_ref[2 * K : 2 * K + 1] = jnp.sqrt(left_over / jnp.where(lane[0:1] < K, norms2, 1.0))

    drain(rows.at[pl.ds(0, NZ - 1)], z_send.at[0])
    drain(rows.at[pl.ds(0, 2 * NS - NZ)], x_send.at[0])
    drain(parts.at[pl.ds(0, NS - 1)], part_send.at[0])
    for sem, buf, count in ((0, tgt_p, NT), (1, tgt_g, NT), (2, plane_p, NS), (3, plane_s, NS), (4, tgt_s, NT)):
        drain(buf.at[pl.ds(0, count - 1)], small_send.at[sem])


def finish(packed_ref, sigma_ref, residual_ref, norms_ref):
    sigma_ref[...] = packed_ref[0:K]
    residual_ref[...] = packed_ref[K : 2 * K]
    norms_ref[...] = packed_ref[2 * K : 2 * K + 1, 0:K]


def shards(trial_vectors, couplings, neighbours, live_slots, energies):
    hbm = pl.BlockSpec(memory_space=pltpu.HBM)
    vmem = pl.BlockSpec(memory_space=pltpu.VMEM)
    dma = pltpu.SemaphoreType.DMA
    packed = pl.pallas_call(
        kernel,
        out_shape=jax.ShapeDtypeStruct((3 * K, S), F32),
        in_specs=[hbm] * 5,
        out_specs=vmem,
        scratch_shapes=[
            pltpu.VMEM((K, S), F32),
            pltpu.VMEM((1, S), F32),
            pltpu.VMEM((NS, S, S), F32),
            pltpu.VMEM((NS, S, 2 * S), BF16),
            pltpu.SMEM((1, NS), jnp.int32),
            pltpu.SMEM((1, NS), jnp.int32),
            pltpu.VMEM((64, K, S), F32),
            pltpu.VMEM((NS, K, S), F32),
            pltpu.VMEM((NS, K, S), F32),
            pltpu.VMEM((8, S), F32),
            pltpu.VMEM((8, S), F32),
            pltpu.VMEM((8, S), F32),
            pltpu.VMEM((8, S), F32),
            pltpu.VMEM((8, S), F32),
            pltpu.VMEM((NT, S), F32),
            pltpu.VMEM((NS, S), F32),
            pltpu.VMEM((NT, S), F32),
            pltpu.VMEM((NS, S), F32),
            pltpu.VMEM((NT, S), F32),
            dma((4,)),
            dma((NS // CHUNK,)),
            dma((1,)),
            dma((NZ,)),
            dma((1,)),
            dma((1,)),
            dma((1,)),
            dma((1,)),
            dma((5,)),
            dma((5,)),
        ],
        compiler_params=pltpu.CompilerParams(collective_id=0, has_side_effects=True),
        name="davidson",
    )(
        trial_vectors.reshape(K, S),
        couplings.reshape(NS, S, S),
        neighbours.reshape(1, NS),
        live_slots.reshape(1, NS),
        energies,
    )
    sigma, residual, norms = pl.pallas_call(
        finish,
        out_shape=(
            jax.ShapeDtypeStruct((K, S), F32),
            jax.ShapeDtypeStruct((K, S), F32),
            jax.ShapeDtypeStruct((1, K), F32),
        ),
        in_specs=[vmem],
        out_specs=(vmem, vmem, vmem),
        name="finish",
    )(packed)
    return sigma.reshape(K, 1, S), residual.reshape(K, 1, S), norms.reshape(K)


def solution(mesh):
    return jax.shard_map(
        shards,
        mesh=mesh,
        in_specs=(
            P(None, ("tgt", "src"), None),
            P("tgt", "src", None, None),
            P("tgt", "src"),
            P("tgt", "src"),
            P(("tgt", "src"), None),
        ),
        out_specs=(P(None, ("tgt", "src"), None), P(None, ("tgt", "src"), None), P()),
        check_vma=False,
    )
```

time: 51.6 us -> 44.6 us (0.86)
  Pallas kernels: 50.7 us -> 43.8 us
    pallas_call x1, Pallas kernels: 49.4 us -> 42.5 us  [shards(): pl.pallas_call(kernel, out_shape=jax.ShapeDtypeStruct((3 * K, S), F32), i...]
where the time goes in v3:
time: 44.6 us; the launch traced here: 44.4 us
  Pallas kernels  43.8 us (98%)
  between operations  0.64 us (1%)
    pallas_call x1, Pallas kernels, shards(): pl.pallas_call(kernel, out_shape=jax.ShapeDtypeStruct((3 * K, S), F32), i...  42.5 us
    pallas_call x1, Pallas kernels, shards(): pl.pallas_call(finish, out_shape=(jax.ShapeDtypeStruct((K, S), F32), jax....  1.31 us

profile of v3, /device:TPU:1, one launch (start us, length us, event | category | flops | bytes accessed | tf_op | source)
XLA Modules:
  0.0 44.4 jit_solution(16877455099768659951)
XLA Ops:
  0.6 42.5 %davidson.1.packed_ref = f32[24,128]{1,0:T(8,128)} custom-call(f32[8,128]{1,0:T(8,128)} %bitcast.12, f32[32,128,128]{2,1,0:T(8,128)} %bitcast.11, s32[1,32]{1,0:T(1,128)} %bitcast.13, s32[1,32]{1,0:T(1,128)} %bitcast.14, f32[1,128]{1,0:T(1,128)} %energies_hbm.1), custom_call_target="tpu_custom_call" | custom-call | tf_op jit(solution)/shard_map/davidson/pallas_call | solution.py:346
  43.1 1.3 %finish.1 = (f32[8,128]{1,0:T(8,128)}, f32[8,128]{1,0:T(8,128)}, f32[1,8]{1,0:T(1,128)}) custom-call(f32[24,128]{1,0:T(8,128)} %davidson.1.packed_ref), custom_call_target="tpu_custom_call" | custom-call | tf_op jit(solution)/shard_map/finish/pallas_call | solution.py:391

commit v4 on v3

--- a/solution.py
+++ b/solution.py
@@ -35,6 +35,10 @@
     pltpu.make_async_copy(ref, ref, sem).wait()
 
 
+def far_first(n, count):
+    return count // 2 + (1 - 2 * (n % 2)) * ((n + 1) // 2)
+
+
 def as_row(pairs):
     full = jnp.concatenate([pairs, jnp.zeros_like(pairs)], axis=0)
     return lax.dot_general(
@@ -43,10 +47,10 @@
 
 
 def as_row8(tile):
-    full = jnp.concatenate([tile, jnp.zeros((S - K, S), F32)], axis=0)
-    return lax.dot_general(
-        jnp.ones((8, S), F32), full, NT_DIMS, precision=HIGHEST, preferred_element_type=F32
-    )
+    total = jnp.broadcast_to(jnp.sum(tile, axis=1, keepdims=True), (K, S))
+    lane = lax.broadcasted_iota(jnp.int32, (K, S), 1)
+    sub = lax.broadcasted_iota(jnp.int32, (K, S), 0)
+    return jnp.sum(jnp.where(lane == sub, total, 0.0), axis=0, keepdims=True)
 
 
 def as_tile(row):
@@ -116,10 +120,10 @@
         greet(((t + 1) % NT, along_x(d)))
         greet(((t + NT - 1) % NT, along_x(d)))
 
-    lax.fori_loop(1, NZ, lambda d, _: greet((t, along_z(d))), None)
-    lax.fori_loop(0, NX, greet_beside, None)
-    lax.fori_loop(2, NT - 1, lambda d, _: greet(((t + d) % NT, s)), None)
-    lax.fori_loop(1, NX, lambda d, _: greet((t, along_x(d))), None)
+    lax.fori_loop(0, NZ - 1, lambda n, _: greet((t, along_z(far_first(n, NZ)))), None, unroll=True)
+    lax.fori_loop(0, NT - 3, lambda n, _: greet(((t + far_first(n, NT)) % NT, s)), None, unroll=True)
+    lax.fori_loop(0, NX, greet_beside, None, unroll=True)
+    lax.fori_loop(1, NX, lambda d, _: greet((t, along_x(d))), None, unroll=True)
 
     for load in loads[1:]:
         load.start()
@@ -137,10 +141,11 @@
     block = (t % 2) * NS
     mine = block + s
 
-    def send_z(d, _):
-        remote(own, rows.at[mine], z_send.at[0], z_recv.at[z], (t, along_z(d))).start()
-
-    lax.fori_loop(1, NZ, send_z, None)
+    def send_z(n, _):
+        to = (t, along_z(far_first(n, NZ)))
+        remote(own, rows.at[mine], z_send.at[0], z_recv.at[z], to).start()
+
+    lax.fori_loop(0, NZ - 1, send_z, None, unroll=True)
     here = pltpu.make_async_copy(own, rows.at[mine], load_sem.at[0])
     here.start()
 
@@ -148,14 +153,10 @@
         at = block + j * NX + x
         beside = (t + NT - 1 + 2 * (j // 4)) % NT
 
-        def send_beside(d, _):
-            remote(src, rows.at[at], x_send.at[0], x_recv.at[0], (beside, along_x(d))).start()
-
-        def send_x(d, _):
-            remote(src, rows.at[at], x_send.at[0], x_recv.at[0], (t, along_x(d))).start()
-
-        lax.fori_loop(0, NX, send_beside, None)
-        lax.fori_loop(1, NX, send_x, None)
+        for n in range(NX):
+            to = along_x(far_first(n, NX))
+            for plane in (beside, t) if n < NX - 1 else (beside,):
+                remote(src, rows.at[at], x_send.at[0], x_recv.at[0], (plane, to)).start()
 
     forward(own, z)
 
@@ -222,16 +223,16 @@
     row_p[...] = as_row(jnp.concatenate(pairs[::-1], 0))
 
     def send_tgt(src, buf, sem):
-        def one(d, _):
+        def one(n, _):
             remote(
                 src.at[pl.ds(0, 1)],
                 buf.at[pl.ds(t, 1)],
                 small_send.at[sem],
                 small_recv.at[sem],
-                ((t + d) % NT, s),
+                ((t + far_first(n, NT)) % NT, s),
             ).start()
 
-        lax.fori_loop(1, NT, one, None)
+        lax.fori_loop(0, NT - 1, one, None, unroll=True)
         buf[pl.ds(t, 1), :] = src[0:1, :]
 
     def wait_tgt(buf, sem):
@@ -239,20 +240,18 @@
         return jnp.sum(buf[...], axis=0, keepdims=True)
 
     def send_plane(src, buf, sem):
-        def one(d, _):
-            to = ((z + 4 + d // NX) % NZ) * NX + (x + 2 + d % NX) % NX
-
-            @pl.when(to != s)
-            def _():
-                remote(
-                    src.at[pl.ds(0, 1)],
-                    buf.at[pl.ds(s, 1)],
-                    small_send.at[sem],
-                    small_recv.at[sem],
-                    (t, to),
-                ).start()
-
-        lax.fori_loop(0, NS, one, None)
+        def one(n, _):
+            to_z = (z + far_first(n // NX, NZ)) % NZ
+            to_x = (x + far_first(n % NX, NX)) % NX
+            remote(
+                src.at[pl.ds(0, 1)],
+                buf.at[pl.ds(s, 1)],
+                small_send.at[sem],
+                small_recv.at[sem],
+                (t, to_z * NX + to_x),
+            ).start()
+
+        lax.fori_loop(0, NS - 1, one, None, unroll=True)
         buf[pl.ds(s, 1), :] = src[0:1, :]
 
     def wait_plane(buf, sem):
@@ -271,7 +270,7 @@
     drain(sums.at[pl.ds(0, NS - 1)], part_recv.at[0])
     sums[s] = parts[s]
     shifted = jnp.sum(sums[...], axis=0) + diagonal
-    row_s[...] = as_row8(shifted * shifted)
+    row_s[...] = jnp.broadcast_to(as_row8(shifted * shifted), (8, S))
     send_plane(row_s, plane_s, 3)
     packed_ref[2 * K : 3 * K] = jnp.zeros((K, S), F32)
     packed_ref[0:K] = shifted + SHIFT * vector
@@ -323,7 +322,7 @@
     missing = projected - times(mixing, metric)
     taken = as_row8(jnp.where(square_mesh, mixing * (projected + missing), 0.0))
 
-    left_over = jnp.maximum(wait_tgt(tgt_s, 4) - taken[0:1], 0.0)
+    left_over = jnp.maximum(wait_tgt(tgt_s, 4) - taken, 0.0)
     packed_ref[2 * K : 2 * K + 1] = jnp.sqrt(left_over / jnp.where(lane[0:1] < K, norms2, 1.0))
 
     drain(rows.at[pl.ds(0, NZ - 1)], z_send.at[0])
@@ -345,7 +344,7 @@
     dma = pltpu.SemaphoreType.DMA
     packed = pl.pallas_call(
         kernel,
-        out_shape=jax.ShapeDtypeStruct((3 * K, S), F32),
+        out_shape=pltpu.VMEM((3 * K, S), F32),
         in_specs=[hbm] * 5,
         out_specs=vmem,
         scratch_shapes=[
@@ -398,7 +397,7 @@
         in_specs=[vmem],
         out_specs=(vmem, vmem, vmem),
         name="finish",
-    )(packed)
+    )(pltpu.with_memory_space_constraint(packed, pltpu.VMEM))
     return sigma.reshape(K, 1, S), residual.reshape(K, 1, S), norms.reshape(K)
 
 

time: 44.6 us -> 42.6 us (0.955)
  Pallas kernels: 43.8 us -> 41.8 us
    pallas_call x1, Pallas kernels: 42.5 us -> 41.2 us  [shards(): pl.pallas_call(kernel, out_shape=pltpu.VMEM((3 * K, S), F32), in_specs=[h...]
    pallas_call x1, Pallas kernels: 1.31 us -> 0.6 us  [shards(): pl.pallas_call(finish, out_shape=(jax.ShapeDtypeStruct((K, S), F32), jax....]
where the time goes in v4:
time: 42.6 us; the launch traced here: 42.4 us
  Pallas kernels  41.8 us (98%)
  between operations  0.64 us (2%)
    pallas_call x1, Pallas kernels, shards(): pl.pallas_call(kernel, out_shape=pltpu.VMEM((3 * K, S), F32), in_specs=[h...  41.2 us

profile of v4, /device:TPU:1, one launch (start us, length us, event | category | flops | bytes accessed | tf_op | source)
XLA Modules:
  0.0 42.4 jit_solution(2420706407971156719)
XLA Ops:
  0.6 41.2 %davidson.1.packed_ref = f32[24,128]{1,0:T(8,128)S(1)} custom-call(f32[8,128]{1,0:T(8,128)} %bitcast.12, f32[32,128,128]{2,1,0:T(8,128)} %bitcast.11, s32[1,32]{1,0:T(1,128)} %bitcast.13, s32[1,32]{1,0:T(1,128)} %bitcast.14, f32[1,128]{1,0:T(1,128)} %energies_hbm.1), custom_call_target="tpu_custom_call" | custom-call | tf_op jit(solution)/shard_map/davidson/pallas_call | solution.py:345
  41.8 0.6 %finish.1 = (f32[8,128]{1,0:T(8,128)}, f32[8,128]{1,0:T(8,128)}, f32[1,8]{1,0:T(1,128)}) custom-call(f32[24,128]{1,0:T(8,128)S(1)} %davidson.1.packed_ref), custom_call_target="tpu_custom_call" | custom-call | tf_op jit(solution)/shard_map/finish/pallas_call | solution.py:390

commit v5 on v4

--- a/solution.py
+++ b/solution.py
@@ -111,17 +111,17 @@
         pl.semaphore_signal(barrier, inc=1, device_id=device, device_id_type=MESH)
 
     def along_z(d):
-        return ((z + d) % NZ) * NX + x
+        return lax.rem(z + d, NZ) * NX + x
 
     def along_x(d):
-        return z * NX + (x + d) % NX
+        return z * NX + lax.rem(x + d, NX)
 
     def greet_beside(d, _):
-        greet(((t + 1) % NT, along_x(d)))
-        greet(((t + NT - 1) % NT, along_x(d)))
+        greet((lax.rem(t + 1, NT), along_x(d)))
+        greet((lax.rem(t + NT - 1, NT), along_x(d)))
 
     lax.fori_loop(0, NZ - 1, lambda n, _: greet((t, along_z(far_first(n, NZ)))), None, unroll=True)
-    lax.fori_loop(0, NT - 3, lambda n, _: greet(((t + far_first(n, NT)) % NT, s)), None, unroll=True)
+    lax.fori_loop(0, NT - 3, lambda n, _: greet((lax.rem(t + far_first(n, NT), NT), s)), None, unroll=True)
     lax.fori_loop(0, NX, greet_beside, None, unroll=True)
     lax.fori_loop(1, NX, lambda d, _: greet((t, along_x(d))), None, unroll=True)
 
@@ -180,8 +180,13 @@
         forward(row, j)
     drain(rows.at[pl.ds(0, 2 * NS - NZ)], x_recv.at[0])
 
-    def share(i, _):
-        found = rows[index[0, i] % 64] * live[0, i].astype(F32)
+    def target(n):
+        to_z = lax.rem(z + far_first(n // NX, NZ), NZ)
+        return to_z * NX + lax.rem(x + far_first(n % NX, NX), NX)
+
+    def share(n, _):
+        i = target(n)
+        found = rows[lax.rem(index[0, i], 64)] * live[0, i].astype(F32)
         high = found.astype(BF16).astype(F32)
         low = found - high
         left = jnp.concatenate(
@@ -190,19 +195,13 @@
         both = lax.dot_general(left, halves[i], NT_DIMS, preferred_element_type=F32)
         parts[i] = both[0:K] + both[K : 2 * K]
 
-    def send_parts(d):
-        def send_part(e, _):
-            to = ((z + d) % NZ) * NX + (x + e) % NX
-            remote(parts.at[to], sums.at[s], part_send.at[0], part_recv.at[0], (t, to)).start()
-
-        lax.fori_loop(0 if d else 1, NX, send_part, None)
-
-    order = (4, 3, 5, 2, 6, 1, 7, 0)
-    for n, d in enumerate(order):
-        first = ((z + d) % NZ) * NX
-        lax.fori_loop(0, NX, lambda e, _: share(first + e, None), None, unroll=True)
-        if n:
-            send_parts(order[n - 1])
+    def send_part(n, _):
+        to = target(n)
+        remote(parts.at[to], sums.at[s], part_send.at[0], part_recv.at[0], (t, to)).start()
+
+    for first in range(0, NS, 8):
+        lax.fori_loop(first, first + 8, share, None, unroll=True)
+        lax.fori_loop(first, min(first + 8, NS - 1), send_part, None, unroll=True)
 
     def outer(pairs, left, right):
         return tuple(
@@ -215,7 +214,6 @@
     pairs = lax.fori_loop(
         0, NS // 2, lambda i, p: outer(p, rows[block + i], parts[i]), zeros, unroll=8
     )
-    send_parts(order[-1])
     pairs = lax.fori_loop(
         NS // 2, NS, lambda i, p: outer(p, rows[block + i], parts[i]), pairs, unroll=8
     )
@@ -229,7 +227,7 @@
                 buf.at[pl.ds(t, 1)],
                 small_send.at[sem],
                 small_recv.at[sem],
-                ((t + far_first(n, NT)) % NT, s),
+                (lax.rem(t + far_first(n, NT), NT), s),
             ).start()
 
         lax.fori_loop(0, NT - 1, one, None, unroll=True)
@@ -241,8 +239,8 @@
 
     def send_plane(src, buf, sem):
         def one(n, _):
-            to_z = (z + far_first(n // NX, NZ)) % NZ
-            to_x = (x + far_first(n % NX, NX)) % NX
+            to_z = lax.rem(z + far_first(n // NX, NZ), NZ)
+            to_x = lax.rem(x + far_first(n % NX, NX), NX)
             remote(
                 src.at[pl.ds(0, 1)],
                 buf.at[pl.ds(s, 1)],
@@ -322,14 +320,17 @@
     missing = projected - times(mixing, metric)
     taken = as_row8(jnp.where(square_mesh, mixing * (projected + missing), 0.0))
 
-    left_over = jnp.maximum(wait_tgt(tgt_s, 4) - taken, 0.0)
-    packed_ref[2 * K : 2 * K + 1] = jnp.sqrt(left_over / jnp.where(lane[0:1] < K, norms2, 1.0))
+    scale = 1.0 / jnp.where(lane[0:1] < K, norms2, 1.0)
 
     drain(rows.at[pl.ds(0, NZ - 1)], z_send.at[0])
     drain(rows.at[pl.ds(0, 2 * NS - NZ)], x_send.at[0])
     drain(parts.at[pl.ds(0, NS - 1)], part_send.at[0])
-    for sem, buf, count in ((0, tgt_p, NT), (1, tgt_g, NT), (2, plane_p, NS), (3, plane_s, NS), (4, tgt_s, NT)):
+    for sem, buf, count in ((0, tgt_p, NT), (1, tgt_g, NT), (2, plane_p, NS), (3, plane_s, NS)):
         drain(buf.at[pl.ds(0, count - 1)], small_send.at[sem])
+
+    left_over = jnp.maximum(wait_tgt(tgt_s, 4) - taken, 0.0)
+    packed_ref[2 * K : 2 * K + 1] = jnp.sqrt(left_over * scale)
+    drain(tgt_s.at[pl.ds(0, NT - 1)], small_send.at[4])
 
 
 def finish(packed_ref, sigma_ref, residual_ref, norms_ref):

time: 42.6 us -> 42.2 us (level)
  no operation moved by 1% of the time
where the time goes in v5:
time: 42.2 us; the launch traced here: 42.1 us
  Pallas kernels  41.4 us (98%)
  between operations  0.64 us (2%)
    pallas_call x1, Pallas kernels, shards(): pl.pallas_call(kernel, out_shape=pltpu.VMEM((3 * K, S), F32), in_specs=[h...  40.8 us

profile of v5, /device:TPU:1, one launch (start us, length us, event | category | flops | bytes accessed | tf_op | source)
XLA Modules:
  0.0 42.1 jit_solution(9725555186813321128)
XLA Ops:
  0.6 40.8 %davidson.1.packed_ref = f32[24,128]{1,0:T(8,128)S(1)} custom-call(f32[8,128]{1,0:T(8,128)} %bitcast.12, f32[32,128,128]{2,1,0:T(8,128)} %bitcast.11, s32[1,32]{1,0:T(1,128)} %bitcast.13, s32[1,32]{1,0:T(1,128)} %bitcast.14, f32[1,128]{1,0:T(1,128)} %energies_hbm.1), custom_call_target="tpu_custom_call" | custom-call | tf_op jit(solution)/shard_map/davidson/pallas_call | solution.py:346
  41.5 0.6 %finish.1 = (f32[8,128]{1,0:T(8,128)}, f32[8,128]{1,0:T(8,128)}, f32[1,8]{1,0:T(1,128)}) custom-call(f32[24,128]{1,0:T(8,128)S(1)} %davidson.1.packed_ref), custom_call_target="tpu_custom_call" | custom-call | tf_op jit(solution)/shard_map/finish/pallas_call | solution.py:391

commit v6 on v5

--- a/solution.py
+++ b/solution.py
@@ -199,9 +199,9 @@
         to = target(n)
         remote(parts.at[to], sums.at[s], part_send.at[0], part_recv.at[0], (t, to)).start()
 
-    for first in range(0, NS, 8):
-        lax.fori_loop(first, first + 8, share, None, unroll=True)
-        lax.fori_loop(first, min(first + 8, NS - 1), send_part, None, unroll=True)
+    for first, last in ((0, 4), (4, 12), (12, 20), (20, NS)):
+        lax.fori_loop(first, last, share, None, unroll=True)
+        lax.fori_loop(first, min(last, NS - 1), send_part, None, unroll=True)
 
     def outer(pairs, left, right):
         return tuple(

time: 42.2 us -> 42.4 us (level)
  no operation moved by 1% of the time
where the time goes in v6:
time: 42.4 us; the launch traced here: 42.3 us
  Pallas kernels  41.7 us (98%)
  between operations  0.64 us (2%)
    pallas_call x1, Pallas kernels, shards(): pl.pallas_call(kernel, out_shape=pltpu.VMEM((3 * K, S), F32), in_specs=[h...  41.1 us

profile of v6, /device:TPU:1, one launch (start us, length us, event | category | flops | bytes accessed | tf_op | source)
XLA Modules:
  0.0 42.3 jit_solution(15427817622695643965)
XLA Ops:
  0.6 41.1 %davidson.1.packed_ref = f32[24,128]{1,0:T(8,128)S(1)} custom-call(f32[8,128]{1,0:T(8,128)} %bitcast.12, f32[32,128,128]{2,1,0:T(8,128)} %bitcast.11, s32[1,32]{1,0:T(1,128)} %bitcast.13, s32[1,32]{1,0:T(1,128)} %bitcast.14, f32[1,128]{1,0:T(1,128)} %energies_hbm.1), custom_call_target="tpu_custom_call" | custom-call | tf_op jit(solution)/shard_map/davidson/pallas_call | solution.py:346
  41.7 0.6 %finish.1 = (f32[8,128]{1,0:T(8,128)}, f32[8,128]{1,0:T(8,128)}, f32[1,8]{1,0:T(1,128)}) custom-call(f32[24,128]{1,0:T(8,128)S(1)} %davidson.1.packed_ref), custom_call_target="tpu_custom_call" | custom-call | tf_op jit(solution)/shard_map/finish/pallas_call | solution.py:391
